TPU v7x, 32 devices: a whole 2x2x4 slice. The times are simulated.
32 devices in a mesh: prow: 4 (over y, core), pcol: 8 (over z, x).
Axes of the slice: x: 2, y: 2, z: 4, core: 2. Of those that a mesh axis runs over, the one named last changes fastest.
Arguments:
- inverse_tiles: float32 [8, 4096, 512], P('prow', 'pcol'), may hold values from -0.36 to 0.36
- tile_rows: int32 [8, 8], P('prow', 'pcol'), may hold values from -1 to 1, as said below
- panel: float32 [4096, 1024], P(('prow', 'pcol')), may hold values from -0.6 to 0.6
- pivot_base: float32 [1024, 512], P('pcol'), may hold values from -6 to 6
Outputs:
- panel_inverse: float32 [4096, 1024], P(('prow', 'pcol'))
- pivot_inverse: float32 [1024, 512], P('pcol')
Inputs may be any that keep to these rules, and one draw needn't show every extreme that they name: `tile_rows`: on each device the entries name distinct row tiles first and -1 after; the device at prow 0 and pcol 0 lists 2.
All inputs are finite; a program needn't handle non-finite values.
Results may differ from a plain program's by a relative error of at most 0.0003.
Values sent between devices are 32-bit elements; how exact they have to be, the bound alone decides.
A program may use at most 64 MiB of HBM per device.

v0:
```python
import jax
import jax.numpy as jnp
from jax import lax
from jax.sharding import PartitionSpec as P


def local(inverse_tiles, tile_rows, panel, pivot_base):
    block = inverse_tiles.shape[1]
    width = panel.shape[1]
    share = panel.shape[0]
    row_tiles = share * lax.axis_size("pcol") // block
    column = lax.all_gather(panel, "prow", axis=0, tiled=True)
    codes = tile_rows[:, 0]
    count = jnp.sum((codes >= 0).astype(jnp.int32))
    totals = jnp.zeros((row_tiles, block, width - 0), jnp.float32)

    def add_tile(slot, totals):
        tile = lax.dynamic_index_in_dim(inverse_tiles, slot, 0, keepdims=False)
        tile_row = lax.dynamic_index_in_dim(codes, slot, 0, keepdims=False)
        product = jnp.dot(
            tile, column, precision=lax.Precision.HIGHEST, preferred_element_type=jnp.float32
        )
        current = lax.dynamic_index_in_dim(totals, tile_row, 0, keepdims=False)
        return lax.dynamic_update_index_in_dim(totals, current + product, tile_row, 0)

    totals = lax.fori_loop(0, count, add_tile, totals)
    trailing = lax.psum_scatter(
        totals.reshape(row_tiles * block, width - 0), "pcol", scatter_dimension=0, tiled=True
    )
    panel_inverse = -trailing
    upper = panel.reshape(share, width // block, block)
    lower = trailing.reshape(share, width // block, block)
    partial_update = jnp.einsum("rka,rkb->kab", upper, lower, precision=lax.Precision.HIGHEST)
    flat = partial_update.reshape(1, width, block)
    received = lax.all_to_all(flat, "pcol", split_axis=1, concat_axis=0, tiled=True)
    column_part = jnp.sum(received, axis=0)
    mine = lax.psum(column_part, "prow")
    return (panel_inverse, pivot_base + mine)


def solution(mesh):
    return jax.shard_map(
        local,
        mesh=mesh,
        in_specs=(
            P("prow", "pcol", None),
            P("prow", "pcol"),
            P(("prow", "pcol"), None),
            P("pcol", None),
        ),
        out_specs=(P(("prow", "pcol"), None), P("pcol", None)),
        check_vma=False,
    )
```

profile of v0, /device:TPU:0, one launch (start us, length us, event | category | flops | bytes accessed | tf_op | source)
XLA Modules:
  0.0 245.9 jit_solution(12357227214868893500)
XLA Ops:
  7.2 0.7 all-gather.2.cloned.1.call-update
  7.9 1.3 fusion.6
  9.2 25.6 %all-gather.2.cloned.1.call-done = f32[512,1024]{1,0:T(8,128)} async-done(((f32[128,1024]{1,0:T(8,128)}), f32[512,1024]{1,0:T(8,128)}) %all-gather.2.cloned.1.call-update) | async-done | bytes 2097168 | tf_op jit(solution)/shard_map/all_gather | solution.py:12
  34.9 2.5 %broadcast_in_dim.7 = f32[2,512,1024]{2,1,0:T(8,128)} broadcast(f32[]{:T(128)} %constant.18.clone.1), dimensions={} | broadcast | bytes 4194308 | tf_op jit(solution)/shard_map/broadcast_in_dim | solution.py:15
  37.3 21.7 %while.10 = (s32[]{:T(128)}, f32[2,512,1024]{2,1,0:T(8,128)}, s32[]{:T(128)}, s32[2]{0:T(128)S(1)}, f32[2,512,512]{2,1,0:T(8,128)}, /*index=5*/f32[512,1024]{1,0:T(8,128)S(1)}, s32[]{:T(128)}, s32[]{:T(128)}, s32[]{:T(128)}) while((s32[]{:T(128)}, f32[2,512,1024]{2,1,0:T(8,128)}, s32[]{:T(128)}, s32[2]{0:T(128)S(1)}, ...), condition=%wide.region_2.3_spmd, body=%wide.region_1.2_spmd.sunk | while | flops 3221749760 | bytes 19923156 | solution.py:26
  38.0 0.7 dynamic_slice.22
  40.7 1.9 constant_dynamic-slice_fusion.2
  42.6 0.3 copy-done.1
  42.9 5.0 %bitcast_dynamic-update-slice_fusion.2 = f32[2,512,1024]{2,1,0:T(8,128)} fusion(f32[2,512,1024]{2,1,0:T(8,128)} %get-tuple-element.96, s32[]{:T(128)S(6)} %select_n.15, f32[1,512,1024]{2,1,0:T(8,128)S(1)} %constant_dynamic-slice_fusion.2, f32[512,1024]{1,0:T(8,128)S(1)} %get-tuple-element.109, f32[2,512,512]{2,1,0:T(8,128)S(1)} %copy-done.1, ...), kind=kOutput, calls=%fused_computation.clone.1 | convolution fusion | flops 3221749760 | bytes 7340040 | tf_op jit(solution)/shard_map/while/body/dot_general | solution.py:20
  48.5 0.7 dynamic_slice.22
  51.2 1.9 constant_dynamic-slice_fusion.2
  53.1 0.3 copy-done.1
  53.5 5.0 %bitcast_dynamic-update-slice_fusion.2 = f32[2,512,1024]{2,1,0:T(8,128)} fusion(f32[2,512,1024]{2,1,0:T(8,128)} %get-tuple-element.96, s32[]{:T(128)S(6)} %select_n.15, f32[1,512,1024]{2,1,0:T(8,128)S(1)} %constant_dynamic-slice_fusion.2, f32[512,1024]{1,0:T(8,128)S(1)} %get-tuple-element.109, f32[2,512,512]{2,1,0:T(8,128)S(1)} %copy-done.1, ...), kind=kOutput, calls=%fused_computation.clone.1 | convolution fusion | flops 3221749760 | bytes 7340040 | tf_op jit(solution)/shard_map/while/body/dot_general | solution.py:20
  59.2 1.0 copy-done.2
  60.1 0.2 copy.11
  60.3 87.2 %reduce-scatter.2.cloned.1.call-done = f32[128,1024]{1,0:T(8,128)} async-done(((f32[1024,1024]{1,0:T(8,128)}), f32[128,1024]{1,0:T(8,128)}) %reduce-scatter.2.cloned.1.call-update) | async-done | bytes 524304 | tf_op jit(solution)/shard_map/reduce_scatter | solution.py:27
  147.6 2.8 %fusion.3 = f32[2,512,512]{1,2,0:T(8,128)S(1)} fusion(f32[128,2,512]{0,2,1:T(8,128)S(1)} %bitcast.37, f32[16,2,8,512]{3,2,1,0:T(8,128)} %bitcast.36), kind=kOutput, calls=%fused_computation.6 | convolution fusion | flops 805306368 | bytes 3145728 | tf_op jit(solution)/shard_map/rka,rkb->kab/dot_general | solution.py:33
  150.4 2.2 copy.10
  152.6 52.5 %all_to_all.12 = f32[1,1024,512]{2,0,1:T(1,128)S(1)} all-to-all(f32[1,1024,512]{2,0,1:T(1,128)S(1)} %copy.10), channel_id=1, replica_groups=mesh['prow'=4,'pcol'=8] {'pcol'}, dimensions={1} | all-to-all | bytes 4194304 | tf_op jit(solution)/shard_map/all_to_all | solution.py:35
  205.0 0.2 copy.12
  205.2 0.9 reduce_sum.19
  206.2 0.8 neg.3
  207.1 30.5 %all-reduce.2.cloned.1.call-done = f32[128,512]{1,0:T(8,128)} async-done(((f32[128,512]{1,0:T(8,128)}), f32[128,512]{1,0:T(8,128)}) %all-reduce.2.cloned.1.call-update) | async-done | bytes 262160 | tf_op jit(solution)/shard_map/psum | solution.py:37
  237.6 1.7 add.25
  (16 shorter events, 0.3 us)
Async XLA Ops:
  7.2 27.7 %all-gather.2.cloned.1.call-start = ((), (), s32[]{:S(2)}) async-start(), calls=%async_computation.2 | async-start | bytes 2621440 | tf_op jit(solution)/shard_map/all_gather | solution.py:12
  7.9 139.7 %reduce-scatter.2.cloned.1.call-start = ((), (), s32[]{:S(2)}) async-start(), calls=%async_computation.3 | async-start | bytes 4718592 | tf_op jit(solution)/shard_map/reduce_scatter | solution.py:27
  34.9 2.5 %copy-start = (f32[512,1024]{1,0:T(8,128)S(1)}, f32[512,1024]{1,0:T(8,128)}, u32[]{:S(2)}) copy-start(f32[512,1024]{1,0:T(8,128)} %all-gather.2.cloned.1.call-done) | copy-start | bytes 6291460
  34.9 2.5 %copy-start.5 = (s32[2,1]{0,1:T(1,128)S(1)}, s32[2,1]{0,1:T(1,128)}, u32[]{:S(2)}) copy-start(s32[2,1]{0,1:T(1,128)} %param.7) | copy-start | bytes 28
  40.7 2.2 copy-start.1
  51.2 2.2 copy-start.1
  59.1 1.0 copy-start.2
  59.1 178.5 %all-reduce.2.cloned.1.call-start = ((), (), s32[]{:S(2)}) async-start(), calls=%async_computation.4 | async-start | bytes 524288 | tf_op jit(solution)/shard_map/psum | solution.py:37
  205.2 1.0 copy-start.3
  205.2 32.4 %copy-start.4 = (f32[128,512]{1,0:T(8,128)S(1)}, f32[128,512]{1,0:T(8,128)}, u32[]{:S(2)}) copy-start(f32[128,512]{1,0:T(8,128)} %param.9) | copy-start | bytes 786436
Sparse Core Ops, SparseCore 0:
  9.5 25.2 all-gather.1
  59.2 88.2 reduce-scatter.1
  206.3 31.2 all-reduce.1
where the time goes:
time: 246 us
  waiting for transfers between devices  144 us (59%)
  blocking collectives  52.5 us (21%)
  between operations  13.8 us (6%)
  matrix products  12.8 us (5%)
  local copies, waits for them, and re-layouts  11.8 us (5%)
  loops' own time  6.09 us (2%)
  other arithmetic  4.73 us (2%)
    reduce_scatter x1, waiting for transfers between devices, local(): lax.psum_scatter(totals.reshape(row_tiles * block, width - 0), 'pcol', sc...  87.2 us
    all_to_all x1, blocking collectives, local(): lax.all_to_all(flat, 'pcol', split_axis=1, concat_axis=0, tiled=True)  52.5 us
    psum x1, waiting for transfers between devices, local(): mine = lax.psum(column_part, 'prow')  30.5 us
    all_gather x1, waiting for transfers between devices, local(): column = lax.all_gather(panel, 'prow', axis=0, tiled=True)  25.6 us
    dot_general x2, matrix products, add_tile(): jnp.dot(tile, column, precision=lax.Precision.HIGHEST, preferred_element_...  9.93 us
    another operation x1, loops' own time, local(): totals = lax.fori_loop(0, count, add_tile, totals)  6.09 us
  transfers between devices with their start and end apart: 3, of which 3 were waited for; matrix products, arithmetic and copies ran while one was open for 1% of the time, Pallas kernels for 0%

commit v1 on v0

v1 whole, which is shorter than its diff:
```python
import functools

import jax
import jax.numpy as jnp
from jax import lax
from jax.experimental import pallas as pl
from jax.experimental.pallas import tpu as pltpu
from jax.sharding import PartitionSpec as P

F32 = jnp.float32
BF16 = jnp.bfloat16
PAIR = 2


def split(value):
    high = value.astype(BF16)
    return high, (value - high.astype(F32)).astype(BF16)


def dot3(a_hi, a_lo, b_hi, b_lo):
    dot = functools.partial(jnp.dot, preferred_element_type=F32)
    return dot(a_hi, b_hi) + (dot(a_hi, b_lo) + dot(a_lo, b_hi))


def kernel(rows, cols, tiles, codes, panel, base, out_panel, out_pivot,
           col, srecv, crecv, u, ut_hi, ut_lo, a_hi, a_lo, b_hi, b_lo, part, uprecv, dnrecv,
           piv, prec, xrec, yrec, zrec, fin,
           sem_col, sem_sib, sem_x, sem_y, sem_s, sem_u, sem_us, sem_rs, sem_rss,
           sem_p, sem_px, sem_py, sem_pys, sem_pz, sem_pzs, sem_f, sem_fs, sem_l):
    ny, nz = rows // PAIR, cols // PAIR
    slots, groups, _, share, block = tiles.shape
    width = panel.shape[1]
    chunk = block // PAIR
    supers = width // block
    per_tile = groups * PAIR
    zset = nz // ny
    zj = nz // supers
    pr, pc = lax.axis_index("prow"), lax.axis_index("pcol")
    c, y = lax.rem(pr, PAIR), lax.div(pr, PAIR)
    x, z = lax.rem(pc, PAIR), lax.div(pc, PAIR)
    oc, ox = 1 - c, 1 - x

    def dev(yy=None, cc=None, zz=None, xx=None):
        yy = y if yy is None else yy
        cc = c if cc is None else cc
        zz = z if zz is None else zz
        xx = x if xx is None else xx
        return (yy * PAIR + cc, zz * PAIR + xx)

    sib, xp = dev(cc=oc), dev(xx=ox)
    pending = []

    def remote(src, dst, send, recv, device):
        return pltpu.make_async_remote_copy(
            src_ref=src, dst_ref=dst, send_sem=send, recv_sem=recv,
            device_id=device, device_id_type=pl.DeviceIdType.MESH)

    def send(cond, *args):
        pending.append((cond, args))
        if cond is None:
            remote(*args).start()
        else:
            @pl.when(cond)
            def _():
                remote(*args).start()

    def arrive(dst, recv):
        remote(dst, dst, recv, recv, xp).wait_recv()

    other_y = [lax.rem(y + k, ny) for k in range(1, ny)]
    other_z = [lax.rem(z + k, nz) for k in range(1, nz)]

    barrier = pltpu.get_barrier_semaphore()
    peers = [dev(cc=oc), xp]
    for yy in other_y:
        peers += [dev(yy=yy), dev(yy=yy, cc=oc)]
    peers += [dev(zz=zz) for zz in other_z]
    for peer in peers:
        pl.semaphore_signal(barrier, inc=1, device_id=peer, device_id_type=pl.DeviceIdType.MESH)
    pl.semaphore_wait(barrier, len(peers))

    own = col.at[x, pr]
    send(None, panel, own, sem_x.at[0], sem_col.at[x, pr], xp)
    for k, yy in enumerate(other_y):
        send(None, panel, own, sem_y.at[0, k], sem_col.at[x, pr], dev(yy=yy))
    send(z + 1 < nz, panel, u.at[z], sem_us.at[0, z], sem_u.at[z], dev(zz=lax.min(z + 1, nz - 1)))
    send(z > 0, panel, u.at[z], sem_us.at[1, z], sem_u.at[z], dev(zz=lax.max(z - 1, 0)))
    send(None, panel, own, sem_sib.at[0, y], sem_col.at[x, pr], sib)
    send(None, codes, crecv, sem_x.at[1], sem_x.at[2], xp)
    for g in range(groups):
        send(None, tiles.at[:, g, ox], srecv.at[:, g], sem_s.at[0, g], sem_s.at[1, g], xp)
    local = [pltpu.make_async_copy(panel, own, sem_l.at[0]),
             pltpu.make_async_copy(panel, u.at[z], sem_l.at[1])]
    for copy in local:
        copy.start()

    far = col.at[ox, pr]
    arrive(far, sem_col.at[ox, pr])
    for k, yy in enumerate(other_y):
        send(None, far, far, sem_y.at[1, k], sem_col.at[ox, pr], dev(yy=yy))
    send(None, far, far, sem_sib.at[1, y], sem_col.at[ox, pr], sib)
    for yy in other_y:
        p = yy * PAIR + c
        arrive(col.at[x, p], sem_col.at[x, p])
        send(None, col.at[x, p], col.at[x, p], sem_sib.at[0, yy], sem_col.at[x, p], sib)

    def relay(d):
        low, high = lax.max(z - d, 0), lax.min(z + d, nz - 1)

        @pl.when(z - d >= 0)
        def _():
            arrive(u.at[low], sem_u.at[low])
        send((z - d >= 0) & (z + 1 < nz), u.at[low], u.at[low], sem_us.at[0, low], sem_u.at[low],
             dev(zz=lax.min(z + 1, nz - 1)))

        @pl.when(z + d < nz)
        def _():
            arrive(u.at[high], sem_u.at[high])
        send((z + d < nz) & (z > 0), u.at[high], u.at[high], sem_us.at[1, high], sem_u.at[high],
             dev(zz=lax.max(z - 1, 0)))

    relay(1)
    for yy in other_y:
        p = yy * PAIR + c
        arrive(col.at[ox, p], sem_col.at[ox, p])
        send(None, col.at[ox, p], col.at[ox, p], sem_sib.at[1, yy], sem_col.at[ox, p], sib)
    for d in range(2, nz):
        relay(d)
    for xx in (x, ox):
        for yy in range(ny):
            p = yy * PAIR + oc
            arrive(col.at[xx, p], sem_col.at[xx, p])
    for copy in local:
        copy.wait()

    for h, xx in enumerate((x, ox)):
        @pl.loop(0, rows)
        def _(p):
            at = pl.multiple_of(p * share, share)
            for n in range(width // chunk):
                hi, lo = split(col[xx, p, :, n * chunk:(n + 1) * chunk])
                b_hi[n, h, pl.ds(at, share), :] = hi
                b_lo[n, h, pl.ds(at, share), :] = lo
    strip = 128
    for k in range(width // strip):
        piece = u[:, :, k * strip:(k + 1) * strip].reshape(nz * share, strip)
        hi, lo = split(piece.T)
        ut_hi[k * strip:(k + 1) * strip, :] = hi
        ut_lo[k * strip:(k + 1) * strip, :] = lo

    def place(h, source, marks):
        for zz in range(nz):
            level, g = zz * PAIR // per_tile, zz * PAIR % per_tile // PAIR
            total = jnp.zeros((share, block), F32)
            for k in range(slots):
                total += jnp.where(marks[k, 0:1, :] == level, source(k, g), 0.0)
            hi, lo = split(total)
            a_hi[h, zz * share:(zz + 1) * share, :] = hi
            a_lo[h, zz * share:(zz + 1) * share, :] = lo

    place(0, lambda k, g: tiles[k, g, x], codes)
    arrive(crecv, sem_x.at[2])
    for g in range(groups):
        arrive(srecv.at[:, g], sem_s.at[1, g])
    place(1, lambda k, g: srecv[k, g], crecv)

    up, down = dev(zz=lax.min(z + 1, nz - 1)), dev(zz=lax.max(z - 1, 0))

    def up_args(n, t):
        return (part.at[n, t], uprecv.at[n, t], sem_rss.at[n, t], sem_rs.at[0, n, t], up)

    def down_args(n, t):
        return (part.at[n, t], dnrecv.at[n, t], sem_rss.at[n, t], sem_rs.at[1, n, t], down)

    def sib_args(j):
        at = pl.ds(j * zj, zj)
        return (piv.at[oc, at], prec.at[at], sem_p.at[0, j], sem_p.at[1, j], sib)

    @pl.loop(0, supers)
    def _(j):
        for half in range(PAIR):
            n = j * PAIR + half
            product = (dot3(a_hi[0], a_lo[0], b_hi[n, 0], b_lo[n, 0])
                       + dot3(a_hi[1], a_lo[1], b_hi[n, 1], b_lo[n, 1]))
            part[n] = product.reshape(nz, share, chunk)
            for t in range(1, nz):
                @pl.when(z == 0)
                def _():
                    remote(*up_args(n, nz - t)).start()

                @pl.when(z == nz - 1)
                def _():
                    remote(*down_args(n, t - 1)).start()
            hi, lo = split(product)
            at = pl.ds(pl.multiple_of(j * block, block), block)
            update = dot3(ut_hi[at, :], ut_lo[at, :], hi, lo)
            piv[half, pl.ds(j * zj, zj)] = update.reshape(zj, PAIR, base.shape[0], chunk)
        remote(*sib_args(j)).start()

    for j in range(supers):
        pending.append((None, sib_args(j)))
    for n in range(width // chunk):
        for t in range(nz):
            pending.append((z < t, up_args(n, t)))
            pending.append((z > t, down_args(n, t)))

    def pass_on(n):
        for k in range(1, nz):
            t, b = nz - k, k - 1

            @pl.when((z > 0) & (z < t))
            def _():
                arrive(uprecv.at[n, t], sem_rs.at[0, n, t])
                part[n, t] = part[n, t] + uprecv[n, t]
                remote(*up_args(n, t)).start()

            @pl.when((z < nz - 1) & (z > b))
            def _():
                arrive(dnrecv.at[n, b], sem_rs.at[1, n, b])
                part[n, b] = part[n, b] + dnrecv[n, b]
                remote(*down_args(n, b)).start()

    def pivot_pair():
        for j in range(supers):
            at = pl.ds(j * zj, zj)
            arrive(prec.at[at], sem_p.at[1, j])
            piv[c, at] = piv[c, at] + prec[at]
            send(None, piv.at[c, at, ox], xrec.at[at], sem_px.at[0, j], sem_px.at[1, j], xp)

    def pivot_x():
        for j in range(supers):
            at = pl.ds(j * zj, zj)
            arrive(xrec.at[at], sem_px.at[1, j])
            piv[c, at, x] = piv[c, at, x] + xrec[at]
        for k, yy in enumerate(other_y):
            send(None, piv.at[c, pl.ds(yy * zset, zset), x], yrec.at[y], sem_pys.at[k], sem_py.at[y],
                 dev(yy=yy))

    mine = lax.div(z, zset) == y

    def pivot_y():
        at = pl.ds(y * zset, zset)
        for yy in other_y:
            arrive(yrec.at[yy], sem_py.at[yy])
            piv[c, at, x] = piv[c, at, x] + yrec[yy]
        for k in range(zset):
            t = y * zset + k
            send(t != z, piv.at[c, t, x], zrec.at[z], sem_pzs.at[k], sem_pz.at[z],
                 dev(zz=jnp.where(t != z, t, lax.rem(z + 1, nz))))

    def pivot_z():
        @pl.when(mine)
        def _():
            total = piv[c, z, x]
            for zz in other_z:
                arrive(zrec.at[zz], sem_pz.at[zz])
                total = total + zrec[zz]
            fin[c] = total
        send(mine, fin.at[c], fin.at[c], sem_fs.at[0], sem_f.at[c], sib)
        for k, yy in enumerate(other_y):
            for m, cc in enumerate((c, oc)):
                send(mine, fin.at[c], fin.at[c], sem_fs.at[1 + k * PAIR + m], sem_f.at[c],
                     dev(yy=yy, cc=cc))

    stages = [pivot_pair, pivot_x, pivot_y]
    for n in range(width // chunk):
        pass_on(n)
        if stages:
            stages.pop(0)()
    pivot_z()

    for n in range(width // chunk):
        at = slice(n * chunk, (n + 1) * chunk)
        out_panel[:, at] = -part[n, z]

        @pl.when(z > 0)
        def _():
            arrive(uprecv.at[n, z], sem_rs.at[0, n, z])
            out_panel[:, at] = out_panel[:, at] - uprecv[n, z]

        @pl.when(z < nz - 1)
        def _():
            arrive(dnrecv.at[n, z], sem_rs.at[1, n, z])
            out_panel[:, at] = out_panel[:, at] - dnrecv[n, z]

    @pl.when(jnp.logical_not(mine))
    def _():
        arrive(fin.at[c], sem_f.at[c])
    arrive(fin.at[oc], sem_f.at[oc])
    for half in range(PAIR):
        at = slice(half * chunk, (half + 1) * chunk)
        out_pivot[:, at] = base[:, at] + fin[half]

    for cond, args in pending:
        if cond is None:
            remote(*args).wait_send()
        else:
            @pl.when(cond)
            def _():
                remote(*args).wait_send()


def local(rows, cols, inverse_tiles, tile_rows, panel, pivot_base):
    slots, block, _ = inverse_tiles.shape
    share, width = panel.shape
    own_rows = pivot_base.shape[0]
    ny, nz = rows // PAIR, cols // PAIR
    chunk = block // PAIR
    chunks = width // chunk
    supers = width // block
    groups = block // share // PAIR
    zset = nz // ny
    tiles = inverse_tiles.reshape(slots, groups, PAIR, share, block)
    codes = jnp.broadcast_to(tile_rows[:, :, None], (slots, 8, block))
    dma, vmem = pltpu.SemaphoreType.DMA, pltpu.VMEM
    deep, tall = PAIR * block, nz * share
    return pl.pallas_call(
        functools.partial(kernel, rows, cols),
        out_shape=(jax.ShapeDtypeStruct((share, width), F32),
                   jax.ShapeDtypeStruct((own_rows, block), F32)),
        in_specs=[pl.BlockSpec(memory_space=pltpu.VMEM)] * 4,
        out_specs=[pl.BlockSpec(memory_space=pltpu.VMEM)] * 2,
        scratch_shapes=[
            vmem((PAIR, rows, share, width), F32),
            vmem((slots, groups, share, block), F32),
            vmem((slots, 8, block), jnp.int32),
            vmem((nz, share, width), F32),
            vmem((width, tall), BF16), vmem((width, tall), BF16),
            vmem((PAIR, tall, block), BF16), vmem((PAIR, tall, block), BF16),
            vmem((chunks, PAIR, block, chunk), BF16), vmem((chunks, PAIR, block, chunk), BF16),
            vmem((chunks, nz, share, chunk), F32),
            vmem((chunks, nz, share, chunk), F32),
            vmem((chunks, nz, share, chunk), F32),
            vmem((PAIR, nz, PAIR, own_rows, chunk), F32),
            vmem((nz, PAIR, own_rows, chunk), F32),
            vmem((nz, own_rows, chunk), F32),
            vmem((ny, zset, own_rows, chunk), F32),
            vmem((nz, own_rows, chunk), F32),
            vmem((PAIR, own_rows, chunk), F32),
            dma((PAIR, rows)), dma((PAIR, ny)), dma((3,)), dma((PAIR, ny)), dma((2, groups)),
            dma((nz,)), dma((2, nz)), dma((2, chunks, nz)), dma((chunks, nz)),
            dma((2, supers)), dma((2, supers)), dma((ny,)), dma((ny,)), dma((nz,)), dma((zset,)),
            dma((PAIR,)), dma((rows,)), dma((2,)),
        ],
        compiler_params=pltpu.CompilerParams(collective_id=0, has_side_effects=True),
    )(tiles, codes, panel, pivot_base)


def solution(mesh):
    return jax.shard_map(
        functools.partial(local, mesh.shape["prow"], mesh.shape["pcol"]),
        mesh=mesh,
        in_specs=(
            P("prow", "pcol", None),
            P("prow", "pcol"),
            P(("prow", "pcol"), None),
            P("pcol", None),
        ),
        out_specs=(P(("prow", "pcol"), None), P("pcol", None)),
        check_vma=False,
    )
```

time: 246 us -> 110 us (0.45)
  waiting for transfers between devices: 144 us -> 0 us
  Pallas kernels: 0 us -> 104 us
  blocking collectives: 52.5 us -> 0 us
  between operations: 13.8 us -> 0.64 us
  matrix products: 12.8 us -> 0 us
  local copies, waits for them, and re-layouts: 11.8 us -> 4.9 us
  loops' own time: 6.09 us -> 0 us
  other arithmetic: 4.73 us -> 0 us
    pallas_call x0 -> x1, Pallas kernels: none -> 104 us  [local(): pl.pallas_call(functools.partial(kernel, rows, cols), out_shape=(jax.Shap...]
    reduce_scatter x1 -> x0, waiting for transfers between devices: 87.2 us -> none  [local(): lax.psum_scatter(totals.reshape(row_tiles * block, width - 0), 'pcol', sc...]
    all_to_all x1 -> x0, blocking collectives: 52.5 us -> none  [local(): lax.all_to_all(flat, 'pcol', split_axis=1, concat_axis=0, tiled=True)]
    psum x1 -> x0, waiting for transfers between devices: 30.5 us -> none  [local(): mine = lax.psum(column_part, 'prow')]
    all_gather x1 -> x0, waiting for transfers between devices: 25.6 us -> none  [local(): column = lax.all_gather(panel, 'prow', axis=0, tiled=True)]
    dot_general x3 -> x0, matrix products: 12.8 us -> none  [the longest x2 9.93 us: add_tile(): jnp.dot(tile, column, precision=lax.Precision.HIGHEST, preferred_element_...]
    another operation x1 -> x0, loops' own time: 6.09 us -> none  [local(): totals = lax.fori_loop(0, count, add_tile, totals)]
    dynamic_slice x4 -> x0, local copies, waits for them, and re-layouts: 5.07 us -> none  [the longest x2 3.76 us: add_tile(): current = lax.dynamic_index_in_dim(totals, tile_row, 0, keepdims=False)]
  transfers between devices with their start and end apart: 3 -> 0, of which waited for: 3 -> 0; matrix products, arithmetic and copies ran while one was open for 1% -> 0% of each run, Pallas kernels for 0% -> 0%
where the time goes in v1:
time: 110 us; the launch traced here: 109 us
  Pallas kernels  104 us (95%)
  local copies, waits for them, and re-layouts  4.9 us (4%)
    pallas_call x1, Pallas kernels, local(): pl.pallas_call(functools.partial(kernel, rows, cols), out_shape=(jax.Shap...  104 us
    unnamed x2, local copies, waits for them, and re-layouts  3.56 us

profile of v1, /device:TPU:0, one launch (start us, length us, event | category | flops | bytes accessed | tf_op | source)
XLA Modules:
  0.0 109.5 jit_solution(18346914025042525189)
XLA Ops:
  0.6 1.3 %broadcast_in_dim.9.codes = s32[2,8,512]{2,1,0:T(8,128)} broadcast(s32[2]{0:T(128)} %bitcast.3), dimensions={0} | broadcast | bytes 32776 | tf_op jit(solution)/shard_map/broadcast_in_dim | solution.py:314
  2.0 104.0 %shard_map.59 = (f32[128,1024]{1,0:T(8,128)}, f32[128,512]{1,0:T(8,128)}) custom-call(f32[2,2,2,128,512]{4,3,2,1,0:T(8,128)} %bitcast.2, s32[2,8,512]{2,1,0:T(8,128)} %broadcast_in_dim.9.codes, f32[128,1024]{1,0:T(8,128)} %panel.1, f32[128,512]{1,0:T(8,128)} %base.1), custom_call_target="tpu_custom_call" | custom-call | tf_op jit(solution)/shard_map/pallas_call | solution.py:317
  105.9 1.9 %copy.8 = f32[128,1024]{1,0:T(8,128)} copy(f32[128,1024]{1,0:T(8,128)} %get-tuple-element.4) | data formatting | bytes 1048576
  107.8 1.7 %copy.9 = f32[128,512]{1,0:T(8,128)} copy(f32[128,512]{1,0:T(8,128)} %get-tuple-element.5) | data formatting | bytes 524288

commit v2 on v1

--- a/solution.py
+++ b/solution.py
@@ -23,7 +23,7 @@
 
 
 def kernel(rows, cols, tiles, codes, panel, base, out_panel, out_pivot,
-           col, srecv, crecv, u, ut_hi, ut_lo, a_hi, a_lo, b_hi, b_lo, part, uprecv, dnrecv,
+           col, srecv, crecv, u, ut_hi, ut_lo, a_hi, a_lo, b_hi, b_lo, c_hi, c_lo, part, uprecv, dnrecv,
            piv, prec, xrec, yrec, zrec, fin,
            sem_col, sem_sib, sem_x, sem_y, sem_s, sem_u, sem_us, sem_rs, sem_rss,
            sem_p, sem_px, sem_py, sem_pys, sem_pz, sem_pzs, sem_f, sem_fs, sem_l):
@@ -124,14 +124,13 @@
         p = yy * PAIR + c
         arrive(col.at[ox, p], sem_col.at[ox, p])
         send(None, col.at[ox, p], col.at[ox, p], sem_sib.at[1, yy], sem_col.at[ox, p], sib)
-    for d in range(2, nz):
+    for d in range(2, nz - 1):
         relay(d)
     for xx in (x, ox):
         for yy in range(ny):
             p = yy * PAIR + oc
             arrive(col.at[xx, p], sem_col.at[xx, p])
-    for copy in local:
-        copy.wait()
+    local[0].wait()
 
     for h, xx in enumerate((x, ox)):
         @pl.loop(0, rows)
@@ -141,28 +140,20 @@
                 hi, lo = split(col[xx, p, :, n * chunk:(n + 1) * chunk])
                 b_hi[n, h, pl.ds(at, share), :] = hi
                 b_lo[n, h, pl.ds(at, share), :] = lo
-    strip = 128
-    for k in range(width // strip):
-        piece = u[:, :, k * strip:(k + 1) * strip].reshape(nz * share, strip)
-        hi, lo = split(piece.T)
-        ut_hi[k * strip:(k + 1) * strip, :] = hi
-        ut_lo[k * strip:(k + 1) * strip, :] = lo
-
-    def place(h, source, marks):
-        for zz in range(nz):
-            level, g = zz * PAIR // per_tile, zz * PAIR % per_tile // PAIR
+
+    levels = nz // groups
+
+    def place(h, g, source, marks):
+        for level in range(levels):
             total = jnp.zeros((share, block), F32)
             for k in range(slots):
                 total += jnp.where(marks[k, 0:1, :] == level, source(k, g), 0.0)
             hi, lo = split(total)
-            a_hi[h, zz * share:(zz + 1) * share, :] = hi
-            a_lo[h, zz * share:(zz + 1) * share, :] = lo
-
-    place(0, lambda k, g: tiles[k, g, x], codes)
-    arrive(crecv, sem_x.at[2])
+            a_hi[g, h, level * share:(level + 1) * share, :] = hi
+            a_lo[g, h, level * share:(level + 1) * share, :] = lo
+
     for g in range(groups):
-        arrive(srecv.at[:, g], sem_s.at[1, g])
-    place(1, lambda k, g: srecv[k, g], crecv)
+        place(0, g, lambda k, g: tiles[k, g, x], codes)
 
     up, down = dev(zz=lax.min(z + 1, nz - 1)), dev(zz=lax.max(z - 1, 0))
 
@@ -176,37 +167,47 @@
         at = pl.ds(j * zj, zj)
         return (piv.at[oc, at], prec.at[at], sem_p.at[0, j], sem_p.at[1, j], sib)
 
-    @pl.loop(0, supers)
-    def _(j):
-        for half in range(PAIR):
-            n = j * PAIR + half
-            product = (dot3(a_hi[0], a_lo[0], b_hi[n, 0], b_lo[n, 0])
-                       + dot3(a_hi[1], a_lo[1], b_hi[n, 1], b_lo[n, 1]))
-            part[n] = product.reshape(nz, share, chunk)
-            for t in range(1, nz):
-                @pl.when(z == 0)
-                def _():
-                    remote(*up_args(n, nz - t)).start()
-
-                @pl.when(z == nz - 1)
-                def _():
-                    remote(*down_args(n, t - 1)).start()
-            hi, lo = split(product)
-            at = pl.ds(pl.multiple_of(j * block, block), block)
-            update = dot3(ut_hi[at, :], ut_lo[at, :], hi, lo)
-            piv[half, pl.ds(j * zj, zj)] = update.reshape(zj, PAIR, base.shape[0], chunk)
-        remote(*sib_args(j)).start()
-
-    for j in range(supers):
-        pending.append((None, sib_args(j)))
+    def multiply(g):
+        @pl.loop(0, supers)
+        def _(j):
+            for half in range(PAIR):
+                n = j * PAIR + half
+                product = (dot3(a_hi[g, 0], a_lo[g, 0], b_hi[n, 0], b_lo[n, 0])
+                           + dot3(a_hi[g, 1], a_lo[g, 1], b_hi[n, 1], b_lo[n, 1]))
+                hi, lo = split(product)
+                for level in range(levels):
+                    at = slice(level * share, (level + 1) * share)
+                    t = level * groups + g
+                    part[n, t] = product[at]
+                    c_hi[n, t * share:(t + 1) * share, :] = hi[at]
+                    c_lo[n, t * share:(t + 1) * share, :] = lo[at]
+                for level in range(levels):
+                    t, b = (levels - 1 - level) * groups + g, level * groups + g
+                    if t > 1:
+                        @pl.when(z == 0)
+                        def _():
+                            remote(*up_args(n, t)).start()
+                    if b < nz - 2:
+                        @pl.when(z == nz - 1)
+                        def _():
+                            remote(*down_args(n, b)).start()
+
+    def update(n):
+        j, half = n // PAIR, n % PAIR
+        at = slice(j * block, (j + 1) * block)
+        value = dot3(ut_hi[at, :], ut_lo[at, :], c_hi[n], c_lo[n])
+        piv[half, j * zj:(j + 1) * zj] = value.reshape(zj, PAIR, base.shape[0], chunk)
+        if half == PAIR - 1:
+            send(None, *sib_args(j))
+
     for n in range(width // chunk):
         for t in range(nz):
             pending.append((z < t, up_args(n, t)))
             pending.append((z > t, down_args(n, t)))
 
-    def pass_on(n):
-        for k in range(1, nz):
-            t, b = nz - k, k - 1
+    def pass_on(n, g):
+        for level in range(levels):
+            t, b = (levels - 1 - level) * groups + g, level * groups + g
 
             @pl.when((z > 0) & (z < t))
             def _():
@@ -262,9 +263,42 @@
                 send(mine, fin.at[c], fin.at[c], sem_fs.at[1 + k * PAIR + m], sem_f.at[c],
                      dev(yy=yy, cc=cc))
 
+    chunks = width // chunk
+    done = [0] * groups
+    for g in range(groups):
+        if g > 0:
+            for n in range(chunks // 2):
+                pass_on(n, g - 1)
+            done[g - 1] = chunks // 2
+        else:
+            arrive(crecv, sem_x.at[2])
+        arrive(srecv.at[:, g], sem_s.at[1, g])
+        place(1, g, lambda k, g: srecv[k, g], crecv)
+        multiply(g)
+    for n in range(chunks):
+        @pl.when(z == 0)
+        def _():
+            remote(*up_args(n, 1)).start()
+
+        @pl.when(z == nz - 1)
+        def _():
+            remote(*down_args(n, nz - 2)).start()
+    relay(nz - 1)
+    local[1].wait()
+    strip = 128
+    for k in range(width // strip):
+        piece = u[:, :, k * strip:(k + 1) * strip].reshape(nz * share, strip)
+        hi, lo = split(piece.T)
+        ut_hi[k * strip:(k + 1) * strip, :] = hi
+        ut_lo[k * strip:(k + 1) * strip, :] = lo
+    for n in range(chunks):
+        for g in range(groups - 1):
+            if n >= done[g]:
+                pass_on(n, g)
+        update(n)
     stages = [pivot_pair, pivot_x, pivot_y]
-    for n in range(width // chunk):
-        pass_on(n)
+    for n in range(chunks):
+        pass_on(n, groups - 1)
         if stages:
             stages.pop(0)()
     pivot_z()
@@ -326,8 +360,10 @@
             vmem((slots, 8, block), jnp.int32),
             vmem((nz, share, width), F32),
             vmem((width, tall), BF16), vmem((width, tall), BF16),
-            vmem((PAIR, tall, block), BF16), vmem((PAIR, tall, block), BF16),
+            vmem((groups, PAIR, tall // groups, block), BF16),
+            vmem((groups, PAIR, tall // groups, block), BF16),
             vmem((chunks, PAIR, block, chunk), BF16), vmem((chunks, PAIR, block, chunk), BF16),
+            vmem((chunks, tall, chunk), BF16), vmem((chunks, tall, chunk), BF16),
             vmem((chunks, nz, share, chunk), F32),
             vmem((chunks, nz, share, chunk), F32),
             vmem((chunks, nz, share, chunk), F32),

time: 110 us -> 102 us (0.927); the launches traced: 109 us -> 100 us
  Pallas kernels: 104 us -> 94.8 us
    pallas_call x1, Pallas kernels: 104 us -> 94.8 us  [local(): pl.pallas_call(functools.partial(kernel, rows, cols), out_shape=(jax.Shap...]
where the time goes in v2:
time: 102 us; the launch traced here: 100 us
  Pallas kernels  94.8 us (93%)
  local copies, waits for them, and re-layouts  4.9 us (5%)
    pallas_call x1, Pallas kernels, local(): pl.pallas_call(functools.partial(kernel, rows, cols), out_shape=(jax.Shap...  94.8 us
    unnamed x2, local copies, waits for them, and re-layouts  3.56 us

profile of v2, /device:TPU:0, one launch (start us, length us, event | category | flops | bytes accessed | tf_op | source)
XLA Modules:
  0.0 100.3 jit_solution(5183740059092591020)
XLA Ops:
  0.6 1.3 %broadcast_in_dim.9.codes = s32[2,8,512]{2,1,0:T(8,128)} broadcast(s32[2]{0:T(128)} %bitcast.3), dimensions={0} | broadcast | bytes 32776 | tf_op jit(solution)/shard_map/broadcast_in_dim | solution.py:348
  2.0 94.8 %shard_map.59 = (f32[128,1024]{1,0:T(8,128)}, f32[128,512]{1,0:T(8,128)}) custom-call(f32[2,2,2,128,512]{4,3,2,1,0:T(8,128)} %bitcast.2, s32[2,8,512]{2,1,0:T(8,128)} %broadcast_in_dim.9.codes, f32[128,1024]{1,0:T(8,128)} %panel.1, f32[128,512]{1,0:T(8,128)} %base.1), custom_call_target="tpu_custom_call" | custom-call | tf_op jit(solution)/shard_map/pallas_call | solution.py:351
  96.8 1.9 %copy.8 = f32[128,1024]{1,0:T(8,128)} copy(f32[128,1024]{1,0:T(8,128)} %get-tuple-element.4) | data formatting | bytes 1048576
  98.7 1.7 %copy.9 = f32[128,512]{1,0:T(8,128)} copy(f32[128,512]{1,0:T(8,128)} %get-tuple-element.5) | data formatting | bytes 524288

commit v3 on v2

--- a/solution.py
+++ b/solution.py
@@ -221,33 +221,68 @@
                 part[n, b] = part[n, b] + dnrecv[n, b]
                 remote(*down_args(n, b)).start()
 
-    def pivot_pair():
-        for j in range(supers):
-            at = pl.ds(j * zj, zj)
-            arrive(prec.at[at], sem_p.at[1, j])
-            piv[c, at] = piv[c, at] + prec[at]
-            send(None, piv.at[c, at, ox], xrec.at[at], sem_px.at[0, j], sem_px.at[1, j], xp)
-
-    def pivot_x():
-        for j in range(supers):
-            at = pl.ds(j * zj, zj)
-            arrive(xrec.at[at], sem_px.at[1, j])
+    def x_first(j):
+        return j % 2 == 0
+
+    def y_args(j, k, m, to, sender):
+        t = j * zj + k * ny + to
+        if x_first(j):
+            return (piv.at[c, t, x], yrec.at[sender, j, k, 0], sem_pys.at[m, j, k], sem_py.at[sender, j, k],
+                    dev(yy=to))
+        return (piv.at[c, t], yrec.at[sender, j, k], sem_pys.at[m, j, k], sem_py.at[sender, j, k],
+                dev(yy=to))
+
+    def send_y(j):
+        for m, yy in enumerate(other_y):
+            for k in range(zset // supers):
+                send(None, *y_args(j, k, m, yy, y))
+
+    def add_y(j):
+        for yy in other_y:
+            for k in range(zset // supers):
+                t = j * zj + k * ny + y
+                if x_first(j):
+                    arrive(yrec.at[yy, j, k, 0], sem_py.at[yy, j, k])
+                    piv[c, t, x] = piv[c, t, x] + yrec[yy, j, k, 0]
+                else:
+                    arrive(yrec.at[yy, j, k], sem_py.at[yy, j, k])
+                    piv[c, t] = piv[c, t] + yrec[yy, j, k]
+
+    def pivot_pair(j):
+        at = pl.ds(j * zj, zj)
+        arrive(prec.at[at], sem_p.at[1, j])
+        piv[c, at] = piv[c, at] + prec[at]
+        if x_first(j):
+            send(None, piv.at[c, at, ox], xrec.at[at], sem_px.at[0, j * zj], sem_px.at[1, j * zj], xp)
+        else:
+            send_y(j)
+
+    def pivot_one(j):
+        at = pl.ds(j * zj, zj)
+        if x_first(j):
+            arrive(xrec.at[at], sem_px.at[1, j * zj])
             piv[c, at, x] = piv[c, at, x] + xrec[at]
-        for k, yy in enumerate(other_y):
-            send(None, piv.at[c, pl.ds(yy * zset, zset), x], yrec.at[y], sem_pys.at[k], sem_py.at[y],
-                 dev(yy=yy))
-
-    mine = lax.div(z, zset) == y
-
-    def pivot_y():
-        at = pl.ds(y * zset, zset)
-        for yy in other_y:
-            arrive(yrec.at[yy], sem_py.at[yy])
-            piv[c, at, x] = piv[c, at, x] + yrec[yy]
-        for k in range(zset):
-            t = y * zset + k
-            send(t != z, piv.at[c, t, x], zrec.at[z], sem_pzs.at[k], sem_pz.at[z],
+            send_y(j)
+        else:
+            add_y(j)
+            for k in range(zset // supers):
+                t = j * zj + k * ny + y
+                send(None, piv.at[c, t, ox], xrec.at[t], sem_px.at[0, t], sem_px.at[1, t], xp)
+
+    def pivot_two(j):
+        if x_first(j):
+            add_y(j)
+        else:
+            for k in range(zset // supers):
+                t = j * zj + k * ny + y
+                arrive(xrec.at[t], sem_px.at[1, t])
+                piv[c, t, x] = piv[c, t, x] + xrec[t]
+        for k in range(zset // supers):
+            t = j * zj + k * ny + y
+            send(t != z, piv.at[c, t, x], zrec.at[z], sem_pzs.at[j, k], sem_pz.at[z],
                  dev(zz=jnp.where(t != z, t, lax.rem(z + 1, nz))))
+
+    mine = lax.rem(z, ny) == y
 
     def pivot_z():
         @pl.when(mine)
@@ -257,11 +292,13 @@
                 arrive(zrec.at[zz], sem_pz.at[zz])
                 total = total + zrec[zz]
             fin[c] = total
-        send(mine, fin.at[c], fin.at[c], sem_fs.at[0], sem_f.at[c], sib)
         for k, yy in enumerate(other_y):
-            for m, cc in enumerate((c, oc)):
-                send(mine, fin.at[c], fin.at[c], sem_fs.at[1 + k * PAIR + m], sem_f.at[c],
-                     dev(yy=yy, cc=cc))
+            send(mine, fin.at[c], fin.at[c], sem_fs.at[1 + k], sem_f.at[c], dev(yy=yy))
+
+        @pl.when(jnp.logical_not(mine))
+        def _():
+            arrive(fin.at[c], sem_f.at[c])
+        send(None, fin.at[c], fin.at[c], sem_fs.at[0], sem_f.at[c], sib)
 
     chunks = width // chunk
     done = [0] * groups
@@ -296,12 +333,15 @@
             if n >= done[g]:
                 pass_on(n, g)
         update(n)
-    stages = [pivot_pair, pivot_x, pivot_y]
     for n in range(chunks):
         pass_on(n, groups - 1)
-        if stages:
-            stages.pop(0)()
-    pivot_z()
+        if n < supers:
+            pivot_pair(n)
+        elif n == supers:
+            for j in range(supers):
+                pivot_one(j)
+    for j in range(supers):
+        pivot_two(j)
 
     for n in range(width // chunk):
         at = slice(n * chunk, (n + 1) * chunk)
@@ -317,9 +357,7 @@
             arrive(dnrecv.at[n, z], sem_rs.at[1, n, z])
             out_panel[:, at] = out_panel[:, at] - dnrecv[n, z]
 
-    @pl.when(jnp.logical_not(mine))
-    def _():
-        arrive(fin.at[c], sem_f.at[c])
+    pivot_z()
     arrive(fin.at[oc], sem_f.at[oc])
     for half in range(PAIR):
         at = slice(half * chunk, (half + 1) * chunk)
@@ -370,12 +408,13 @@
             vmem((PAIR, nz, PAIR, own_rows, chunk), F32),
             vmem((nz, PAIR, own_rows, chunk), F32),
             vmem((nz, own_rows, chunk), F32),
-            vmem((ny, zset, own_rows, chunk), F32),
+            vmem((ny, supers, zset // supers, PAIR, own_rows, chunk), F32),
             vmem((nz, own_rows, chunk), F32),
             vmem((PAIR, own_rows, chunk), F32),
             dma((PAIR, rows)), dma((PAIR, ny)), dma((3,)), dma((PAIR, ny)), dma((2, groups)),
             dma((nz,)), dma((2, nz)), dma((2, chunks, nz)), dma((chunks, nz)),
-            dma((2, supers)), dma((2, supers)), dma((ny,)), dma((ny,)), dma((nz,)), dma((zset,)),
+            dma((2, supers)), dma((2, nz)), dma((ny, supers, zset // supers)), dma((ny, supers, zset // supers)),
+            dma((nz,)), dma((supers, zset // supers)),
             dma((PAIR,)), dma((rows,)), dma((2,)),
         ],
         compiler_params=pltpu.CompilerParams(collective_id=0, has_side_effects=True),

time: 102 us -> 94.8 us (0.929)
  the two profiles are of different devices: /device:TPU:0 before, /device:TPU:25 now
where the time goes in v3:
time: 94.8 us; the launch traced here: 94.6 us
  Pallas kernels  89.1 us (94%)
  local copies, waits for them, and re-layouts  4.9 us (5%)
    pallas_call x1, Pallas kernels, local(): pl.pallas_call(functools.partial(kernel, rows, cols), out_shape=(jax.Shap...  89.1 us
    unnamed x2, local copies, waits for them, and re-layouts  3.56 us

profile of v3, /device:TPU:25, one launch (start us, length us, event | category | flops | bytes accessed | tf_op | source)
XLA Modules:
  0.0 94.6 jit_solution(3598815001544812365)
XLA Ops:
  0.6 1.3 %broadcast_in_dim.9.codes = s32[2,8,512]{2,1,0:T(8,128)} broadcast(s32[2]{0:T(128)} %bitcast.3), dimensions={0} | broadcast | bytes 32776 | tf_op jit(solution)/shard_map/broadcast_in_dim | solution.py:386
  2.0 89.1 %shard_map.59 = (f32[128,1024]{1,0:T(8,128)}, f32[128,512]{1,0:T(8,128)}) custom-call(f32[2,2,2,128,512]{4,3,2,1,0:T(8,128)} %bitcast.2, s32[2,8,512]{2,1,0:T(8,128)} %broadcast_in_dim.9.codes, f32[128,1024]{1,0:T(8,128)} %panel.1, f32[128,512]{1,0:T(8,128)} %base.1), custom_call_target="tpu_custom_call" | custom-call | tf_op jit(solution)/shard_map/pallas_call | solution.py:389
  91.0 1.9 %copy.8 = f32[128,1024]{1,0:T(8,128)} copy(f32[128,1024]{1,0:T(8,128)} %get-tuple-element.4) | data formatting | bytes 1048576
  92.9 1.7 %copy.9 = f32[128,512]{1,0:T(8,128)} copy(f32[128,512]{1,0:T(8,128)} %get-tuple-element.5) | data formatting | bytes 524288
